TPU v7x, 256 devices: a whole 4x4x8 slice. The times are simulated.
256 devices in a mesh: cell: 32 (over z, y_hi, core), period: 8 (over x, y_lo).
Axes of the slice: x: 4, y: 4 (y_hi: 2, y_lo: 2; y = y_hi * 2 + y_lo), z: 8, core: 2. Of those that a mesh axis runs over, the one named last changes fastest.
Arguments:
- footprints: float32 [32, 16, 32768], P(None, 'period', 'cell'), may hold values from -16 to 16
- cell_coords: int32 [2, 32768], P(None, 'cell'), may hold values from 0 to 255, as said below
- obs_period: int32 [32], replicated, may hold values from 0 to 15
- temporal_cov: float32 [16, 16], replicated, may hold values from -1.5 to 1.5
Outputs:
- hq_field: float32 [32, 16, 32768], P(None, 'period', 'cell')
- hqh_gram: float32 [32, 32], replicated
Inputs may be any that keep to these rules, and one draw needn't show every extreme that they name: `cell_coords`: cells sit at distinct grid points that together fill the rectangle of first coordinates 0 to 255 and second coordinates 0 to 127.
All inputs are finite; a program needn't handle non-finite values.
Results may differ from a plain program's by a relative error of at most 0.0003.
Values sent between devices are 32-bit elements; how exact they have to be, the bound alone decides.
No kernel may reach another device: no remote copies, remote signals or barrier semaphores. Data moves between devices by JAX's collectives and lax.ppermute only.
A program may use at most 64 MiB of HBM per device.

v0:
```python
import jax
import jax.numpy as jnp
from jax import lax
from jax.sharding import PartitionSpec as P

LENGTH_SCALE = 48.0
BLOCK_LIMIT = 4096


def covariance_tile(first_xy, second_xy):
    delta_x = first_xy[0][:, None] - second_xy[0][None, :]
    delta_y = first_xy[1][:, None] - second_xy[1][None, :]
    return jnp.exp(-jnp.sqrt(delta_x * delta_x + delta_y * delta_y) / LENGTH_SCALE)


def block_size(total_width, unit_width):
    unit_count = total_width // unit_width
    best_count = 1
    for factor in range(1, unit_count + 1):
        if unit_count % factor == 0 and factor * unit_width <= max(BLOCK_LIMIT, unit_width):
            best_count = factor
    return best_count * unit_width


def on_device(footprints, cell_coords, obs_period, temporal_cov):
    obs_count, per_local, cell_local = footprints.shape
    flat_count = obs_count * per_local
    period_first = lax.axis_index("period") * per_local
    period_ids = period_first + jnp.arange(per_local, dtype=jnp.int32)
    keep = (period_ids[None, :, None] <= obs_period[:, None, None]).astype(jnp.float32)
    masked = footprints * keep
    flat_rows = masked.reshape(flat_count, cell_local)
    local_places = cell_coords.astype(jnp.float32)
    empty = jnp.zeros((flat_count, cell_local), jnp.float32)
    piece_rows = lax.all_gather(flat_rows, "cell", axis=1, tiled=True)
    piece_places = lax.all_gather(local_places, "cell", axis=1, tiled=True)
    piece_width = piece_rows.shape[1]
    block_width = block_size(piece_width, cell_local)

    def add_block(block_index, running_sum):
        offset = block_index * block_width
        part_rows = lax.dynamic_slice_in_dim(piece_rows, offset, block_width, 1)
        part_places = lax.dynamic_slice_in_dim(piece_places, offset, block_width, 1)
        tile = covariance_tile(part_places, local_places)
        return running_sum + jnp.dot(
            part_rows, tile, precision=lax.Precision.HIGHEST, preferred_element_type=jnp.float32
        )

    spatial_flat = lax.fori_loop(0, piece_width // block_width, add_block, empty)
    spatial = spatial_flat.reshape(obs_count, per_local, cell_local)
    piece = lax.all_gather(spatial, "period", axis=1, tiled=True)
    weights = lax.dynamic_slice(temporal_cov, (period_first, 0), (per_local, piece.shape[1]))
    hq_field = jnp.einsum("tu,nuj->ntj", weights, piece, precision=lax.Precision.HIGHEST)
    partial_gram = jnp.einsum("ntj,mtj->nm", hq_field, masked, precision=lax.Precision.HIGHEST)
    hqh_gram = lax.psum(partial_gram, ("cell", "period"))
    return (hq_field, hqh_gram)


def solution(mesh):
    return jax.shard_map(
        on_device,
        mesh=mesh,
        in_specs=(P(None, "period", "cell"), P(None, "cell"), P(), P()),
        out_specs=(P(None, "period", "cell"), P()),
        check_vma=False,
    )
```

profile of v0, /device:TPU:1, one launch (start us, length us, event | category | flops | bytes accessed | tf_op | source)
XLA Modules:
  0.0 412.7 jit_solution(13719887616135554057)
XLA Ops:
  7.2 0.0 all-gather.3.cloned.1.call-start
  7.2 0.7 compare_convert_fusion
  8.0 0.1 copy.15
  8.1 1.1 broadcast_multiply_fusion
  9.2 0.9 reshape.51
  10.1 0.0 all-gather.5.cloned.1.call-start
  10.1 0.7 convert_element_type.12
  10.8 47.3 %all_gather.10 = f32[2,32768]{1,0:T(2,128)S(1)} all-gather(f32[2,1024]{1,0:T(2,128)S(1)} %convert_element_type.12), channel_id=1, replica_groups=mesh['cell'=32,'period'=8] {'cell'}, dimensions={1}, use_global_device_ids=true | all-gather | bytes 270336 | tf_op jit(solution)/shard_map/all_gather | solution.py:36
  58.1 58.6 %all-gather.3.cloned.1.call-done = f32[64,32768]{1,0:T(8,128)} async-done(((f32[64,1024]{1,0:T(8,128)}), f32[64,32768]{1,0:T(8,128)}) %all-gather.3.cloned.1.call-update) | async-done | bytes 8388624 | tf_op jit(solution)/shard_map/all_gather | solution.py:35
  116.7 157.3 %while.14 = (s32[]{:T(128)}, f32[64,1024]{1,0:T(8,128)S(1)}, f32[64,32768]{1,0:T(8,128)}, f32[2,32768]{1,0:T(2,128)S(1)}, f32[2,1024]{1,0:T(2,128)S(1)}, /*index...) while((s32[]{:T(128)}, f32[64,1024]{1,0:T(8,128)S(1)}, f32[64,32768]{1,0:T(8,128)}, ...), condition=%wide.region_1.0_spmd.clone, body=%wide.region_0.0_spmd.clone.sunk | while | flops 3250716672 | bytes 1695933 | solution.py:49
  116.7 0.1 constant_dynamic-slice_fusion.2
  116.8 19.5 %fusion.39 = f32[64,1024]{1,0:T(8,128)S(1)} fusion(f32[1024]{0:T(1024)S(1)} %bitcast.22, f32[4096]{0:T(1024)S(1)} %bitcast.20, f32[1024]{0:T(1024)S(1)} %bitcast.21, f32[4096]{0:T(1024)S(1)} %bitcast.19, f32[64,32768]{1,0:T(8,128)} %get-tuple-element.190, s32[]{:T(128)S(6)} %select_n.14, f32[64,1024]{1,0:T(8,128)S(1)} %get-tuple-element.179, ...), kind=kOutput, calls=%fused_computation.15.clone.1 | convolution fusion | flops 3250716672 | bytes 1613829 | tf_op jit(solution)/shard_map/while/body/eval_jaxpr/dot_general | solution.py:45
  136.3 0.1 constant_dynamic-slice_fusion.2
  136.4 19.5 %fusion.39 = f32[64,1024]{1,0:T(8,128)S(1)} fusion(f32[1024]{0:T(1024)S(1)} %bitcast.22, f32[4096]{0:T(1024)S(1)} %bitcast.20, f32[1024]{0:T(1024)S(1)} %bitcast.21, f32[4096]{0:T(1024)S(1)} %bitcast.19, f32[64,32768]{1,0:T(8,128)} %get-tuple-element.190, s32[]{:T(128)S(6)} %select_n.14, f32[64,1024]{1,0:T(8,128)S(1)} %get-tuple-element.179, ...), kind=kOutput, calls=%fused_computation.15.clone.1 | convolution fusion | flops 3250716672 | bytes 1613829 | tf_op jit(solution)/shard_map/while/body/eval_jaxpr/dot_general | solution.py:45
  156.0 0.1 constant_dynamic-slice_fusion.2
  156.1 19.5 %fusion.39 = f32[64,1024]{1,0:T(8,128)S(1)} fusion(f32[1024]{0:T(1024)S(1)} %bitcast.22, f32[4096]{0:T(1024)S(1)} %bitcast.20, f32[1024]{0:T(1024)S(1)} %bitcast.21, f32[4096]{0:T(1024)S(1)} %bitcast.19, f32[64,32768]{1,0:T(8,128)} %get-tuple-element.190, s32[]{:T(128)S(6)} %select_n.14, f32[64,1024]{1,0:T(8,128)S(1)} %get-tuple-element.179, ...), kind=kOutput, calls=%fused_computation.15.clone.1 | convolution fusion | flops 3250716672 | bytes 1613829 | tf_op jit(solution)/shard_map/while/body/eval_jaxpr/dot_general | solution.py:45
  175.6 0.1 constant_dynamic-slice_fusion.2
  175.7 19.5 %fusion.39 = f32[64,1024]{1,0:T(8,128)S(1)} fusion(f32[1024]{0:T(1024)S(1)} %bitcast.22, f32[4096]{0:T(1024)S(1)} %bitcast.20, f32[1024]{0:T(1024)S(1)} %bitcast.21, f32[4096]{0:T(1024)S(1)} %bitcast.19, f32[64,32768]{1,0:T(8,128)} %get-tuple-element.190, s32[]{:T(128)S(6)} %select_n.14, f32[64,1024]{1,0:T(8,128)S(1)} %get-tuple-element.179, ...), kind=kOutput, calls=%fused_computation.15.clone.1 | convolution fusion | flops 3250716672 | bytes 1613829 | tf_op jit(solution)/shard_map/while/body/eval_jaxpr/dot_general | solution.py:45
  195.3 0.1 constant_dynamic-slice_fusion.2
  195.4 19.5 %fusion.39 = f32[64,1024]{1,0:T(8,128)S(1)} fusion(f32[1024]{0:T(1024)S(1)} %bitcast.22, f32[4096]{0:T(1024)S(1)} %bitcast.20, f32[1024]{0:T(1024)S(1)} %bitcast.21, f32[4096]{0:T(1024)S(1)} %bitcast.19, f32[64,32768]{1,0:T(8,128)} %get-tuple-element.190, s32[]{:T(128)S(6)} %select_n.14, f32[64,1024]{1,0:T(8,128)S(1)} %get-tuple-element.179, ...), kind=kOutput, calls=%fused_computation.15.clone.1 | convolution fusion | flops 3250716672 | bytes 1613829 | tf_op jit(solution)/shard_map/while/body/eval_jaxpr/dot_general | solution.py:45
  214.9 0.1 constant_dynamic-slice_fusion.2
  215.0 19.5 %fusion.39 = f32[64,1024]{1,0:T(8,128)S(1)} fusion(f32[1024]{0:T(1024)S(1)} %bitcast.22, f32[4096]{0:T(1024)S(1)} %bitcast.20, f32[1024]{0:T(1024)S(1)} %bitcast.21, f32[4096]{0:T(1024)S(1)} %bitcast.19, f32[64,32768]{1,0:T(8,128)} %get-tuple-element.190, s32[]{:T(128)S(6)} %select_n.14, f32[64,1024]{1,0:T(8,128)S(1)} %get-tuple-element.179, ...), kind=kOutput, calls=%fused_computation.15.clone.1 | convolution fusion | flops 3250716672 | bytes 1613829 | tf_op jit(solution)/shard_map/while/body/eval_jaxpr/dot_general | solution.py:45
  234.6 0.1 constant_dynamic-slice_fusion.2
  234.7 19.5 %fusion.39 = f32[64,1024]{1,0:T(8,128)S(1)} fusion(f32[1024]{0:T(1024)S(1)} %bitcast.22, f32[4096]{0:T(1024)S(1)} %bitcast.20, f32[1024]{0:T(1024)S(1)} %bitcast.21, f32[4096]{0:T(1024)S(1)} %bitcast.19, f32[64,32768]{1,0:T(8,128)} %get-tuple-element.190, s32[]{:T(128)S(6)} %select_n.14, f32[64,1024]{1,0:T(8,128)S(1)} %get-tuple-element.179, ...), kind=kOutput, calls=%fused_computation.15.clone.1 | convolution fusion | flops 3250716672 | bytes 1613829 | tf_op jit(solution)/shard_map/while/body/eval_jaxpr/dot_general | solution.py:45
  254.2 0.1 constant_dynamic-slice_fusion.2
  254.3 19.5 %fusion.39 = f32[64,1024]{1,0:T(8,128)S(1)} fusion(f32[1024]{0:T(1024)S(1)} %bitcast.22, f32[4096]{0:T(1024)S(1)} %bitcast.20, f32[1024]{0:T(1024)S(1)} %bitcast.21, f32[4096]{0:T(1024)S(1)} %bitcast.19, f32[64,32768]{1,0:T(8,128)} %get-tuple-element.190, s32[]{:T(128)S(6)} %select_n.14, f32[64,1024]{1,0:T(8,128)S(1)} %get-tuple-element.179, ...), kind=kOutput, calls=%fused_computation.15.clone.1 | convolution fusion | flops 3250716672 | bytes 1613829 | tf_op jit(solution)/shard_map/while/body/eval_jaxpr/dot_general | solution.py:45
  274.0 0.1 reshape.52
  274.2 0.8 copy.16
  275.0 48.4 %all-gather.5.cloned.1.call-done = f32[32,16,1024]{2,0,1:T(8,128)} async-done(((f32[32,2,1024]{2,0,1:T(8,128)}), f32[32,16,1024]{2,0,1:T(8,128)}) %all-gather.5.cloned.1.call-update) | async-done | bytes 2097168 | tf_op jit(solution)/shard_map/all_gather | solution.py:51
  323.4 3.9 fusion.23
  327.3 0.5 convolution_bitcast_fusion
  327.7 78.1 %psum.7 = f32[32,32]{1,0:T(8,128)} all-reduce(f32[32,32]{1,0:T(8,128)S(1)} %convolution_bitcast_fusion), channel_id=1, replica_groups=mesh['cell'=32,'period'=8] {'cell','period'}, use_global_device_ids=true, to_apply=%region_2.0 | all-reduce | flops 1024 | bytes 8192 | tf_op jit(solution)/shard_map/psum | solution.py:55
  (16 shorter events, 0.1 us)
Async XLA Ops:
  7.2 316.2 %copy-start = (f32[16,16]{1,0:T(8,128)S(1)}, f32[16,16]{1,0:T(8,128)}, u32[]{:S(2)}) copy-start(f32[16,16]{1,0:T(8,128)} %param.9) | copy-start | bytes 3076
  7.2 109.5 %all-gather.3.cloned.1.call-start = ((), (), s32[]{:S(2)}) async-start(), calls=%async_computation | async-start | bytes 8650752 | tf_op jit(solution)/shard_map/all_gather | solution.py:35
  10.1 313.3 %all-gather.5.cloned.1.call-start = ((), (), s32[]{:S(2)}) async-start(), calls=%async_computation.1 | async-start | bytes 2359296 | tf_op jit(solution)/shard_map/all_gather | solution.py:51
  327.3 78.6 %copy-start.1 = (f32[32,2,1024]{2,1,0:T(2,128)}, f32[32,2,1024]{2,1,0:T(2,128)S(1)}, u32[]{:S(2)}) copy-start(f32[32,2,1024]{2,1,0:T(2,128)S(1)} %fusion.23) | copy-start | bytes 786436
Sparse Core Ops, SparseCore 0:
  11.4 105.2 all-gather.2
  275.1 48.2 all-gather.4
where the time goes:
time: 413 us
  matrix products  160 us (39%)
  blocking collectives  125 us (30%)
  waiting for transfers between devices  107 us (26%)
  between operations  14.1 us (3%)
    dot_general x8, matrix products, add_block(): jnp.dot(part_rows, tile, precision=lax.Precision.HIGHEST, preferred_eleme...  156 us
    psum x1, blocking collectives, on_device(): hqh_gram = lax.psum(partial_gram, ('cell', 'period'))  78.1 us
    all_gather x1, waiting for transfers between devices, on_device(): piece_rows = lax.all_gather(flat_rows, 'cell', axis=1, tiled=True)  58.6 us
    all_gather x1, waiting for transfers between devices, on_device(): piece = lax.all_gather(spatial, 'period', axis=1, tiled=True)  48.4 us
    all_gather x1, blocking collectives, on_device(): piece_places = lax.all_gather(local_places, 'cell', axis=1, tiled=True)  47.3 us
  transfers between devices with their start and end apart: 2, of which 2 were waited for; matrix products, arithmetic and copies ran while one was open for 0% of the time, Pallas kernels for 0%

commit v1 on v0

--- a/solution.py
+++ b/solution.py
@@ -52,7 +52,8 @@
     weights = lax.dynamic_slice(temporal_cov, (period_first, 0), (per_local, piece.shape[1]))
     hq_field = jnp.einsum("tu,nuj->ntj", weights, piece, precision=lax.Precision.HIGHEST)
     partial_gram = jnp.einsum("ntj,mtj->nm", hq_field, masked, precision=lax.Precision.HIGHEST)
-    hqh_gram = lax.psum(partial_gram, ("cell", "period"))
+    parts = lax.all_gather(partial_gram, ("cell", "period"))
+    hqh_gram = jnp.sum(parts, axis=0)
     return (hq_field, hqh_gram)
 
 

time: 413 us -> 1060 us (2.57)
  waiting for transfers between devices: 107 us -> 827 us
  blocking collectives: 125 us -> 47.3 us
    all_gather x0 -> x1, waiting for transfers between devices: none -> 720 us  [on_device(): parts = lax.all_gather(partial_gram, ('cell', 'period'))]
    psum x1 -> x0, blocking collectives: 78.1 us -> none  [on_device(): hqh_gram = lax.psum(partial_gram, ('cell', 'period'))]
  transfers between devices with their start and end apart: 2 -> 3, of which waited for: 2 -> 3; matrix products, arithmetic and copies ran while one was open for 0% -> 0% of each run, Pallas kernels for 0% -> 0%
where the time goes in v1:
time: 1060 us
  waiting for transfers between devices  827 us (78%)
  matrix products  161 us (15%)
  blocking collectives  47.3 us (4%)
  between operations  13.8 us (1%)
    all_gather x1, waiting for transfers between devices, on_device(): parts = lax.all_gather(partial_gram, ('cell', 'period'))  720 us
    dot_general x8, matrix products, add_block(): jnp.dot(part_rows, tile, precision=lax.Precision.HIGHEST, preferred_eleme...  156 us
    all_gather x1, waiting for transfers between devices, on_device(): piece_rows = lax.all_gather(flat_rows, 'cell', axis=1, tiled=True)  58.6 us
    all_gather x1, waiting for transfers between devices, on_device(): piece = lax.all_gather(spatial, 'period', axis=1, tiled=True)  48.3 us
    all_gather x1, blocking collectives, on_device(): piece_places = lax.all_gather(local_places, 'cell', axis=1, tiled=True)  47.3 us
  transfers between devices with their start and end apart: 3, of which 3 were waited for; matrix products, arithmetic and copies ran while one was open for 0% of the time, Pallas kernels for 0%

profile of v1, /device:TPU:1, one launch (start us, length us, event | category | flops | bytes accessed | tf_op | source)
XLA Modules:
  0.0 1057.8 jit_solution(2075133454489124433)
XLA Ops:
  7.2 0.7 compare_convert_fusion
  8.0 0.1 copy.15
  8.1 1.1 broadcast_multiply_fusion
  9.2 0.9 reshape.51
  10.1 0.7 convert_element_type.12
  10.8 47.3 %all_gather.16 = f32[2,32768]{1,0:T(2,128)S(1)} all-gather(f32[2,1024]{1,0:T(2,128)S(1)} %convert_element_type.12), channel_id=1, replica_groups=mesh['cell'=32,'period'=8] {'cell'}, dimensions={1}, use_global_device_ids=true | all-gather | bytes 270336 | tf_op jit(solution)/shard_map/all_gather | solution.py:36
  58.1 58.6 %all-gather.5.cloned.1.call-done = f32[64,32768]{1,0:T(8,128)} async-done(((f32[64,1024]{1,0:T(8,128)}), f32[64,32768]{1,0:T(8,128)}) %all-gather.5.cloned.1.call-update) | async-done | bytes 8388624 | tf_op jit(solution)/shard_map/all_gather | solution.py:35
  116.7 157.3 %while.14 = (s32[]{:T(128)}, f32[64,1024]{1,0:T(8,128)S(1)}, f32[64,32768]{1,0:T(8,128)}, f32[2,32768]{1,0:T(2,128)S(1)}, f32[2,1024]{1,0:T(2,128)S(1)}, /*index...) while((s32[]{:T(128)}, f32[64,1024]{1,0:T(8,128)S(1)}, f32[64,32768]{1,0:T(8,128)}, ...), condition=%wide.region_1.0_spmd.clone, body=%wide.region_0.0_spmd.clone.sunk | while | flops 3250716672 | bytes 1695933 | solution.py:49
  116.7 0.1 constant_dynamic-slice_fusion.2
  116.8 19.5 %fusion.39 = f32[64,1024]{1,0:T(8,128)S(1)} fusion(f32[1024]{0:T(1024)S(1)} %bitcast.24, f32[4096]{0:T(1024)S(1)} %bitcast.22, f32[1024]{0:T(1024)S(1)} %bitcast.23, f32[4096]{0:T(1024)S(1)} %bitcast.21, f32[64,32768]{1,0:T(8,128)} %get-tuple-element.190, s32[]{:T(128)S(6)} %select_n.14, f32[64,1024]{1,0:T(8,128)S(1)} %get-tuple-element.179, ...), kind=kOutput, calls=%fused_computation.15.clone.1 | convolution fusion | flops 3250716672 | bytes 1613829 | tf_op jit(solution)/shard_map/while/body/eval_jaxpr/dot_general | solution.py:45
  136.3 0.1 constant_dynamic-slice_fusion.2
  136.4 19.5 %fusion.39 = f32[64,1024]{1,0:T(8,128)S(1)} fusion(f32[1024]{0:T(1024)S(1)} %bitcast.24, f32[4096]{0:T(1024)S(1)} %bitcast.22, f32[1024]{0:T(1024)S(1)} %bitcast.23, f32[4096]{0:T(1024)S(1)} %bitcast.21, f32[64,32768]{1,0:T(8,128)} %get-tuple-element.190, s32[]{:T(128)S(6)} %select_n.14, f32[64,1024]{1,0:T(8,128)S(1)} %get-tuple-element.179, ...), kind=kOutput, calls=%fused_computation.15.clone.1 | convolution fusion | flops 3250716672 | bytes 1613829 | tf_op jit(solution)/shard_map/while/body/eval_jaxpr/dot_general | solution.py:45
  156.0 0.1 constant_dynamic-slice_fusion.2
  156.1 19.5 %fusion.39 = f32[64,1024]{1,0:T(8,128)S(1)} fusion(f32[1024]{0:T(1024)S(1)} %bitcast.24, f32[4096]{0:T(1024)S(1)} %bitcast.22, f32[1024]{0:T(1024)S(1)} %bitcast.23, f32[4096]{0:T(1024)S(1)} %bitcast.21, f32[64,32768]{1,0:T(8,128)} %get-tuple-element.190, s32[]{:T(128)S(6)} %select_n.14, f32[64,1024]{1,0:T(8,128)S(1)} %get-tuple-element.179, ...), kind=kOutput, calls=%fused_computation.15.clone.1 | convolution fusion | flops 3250716672 | bytes 1613829 | tf_op jit(solution)/shard_map/while/body/eval_jaxpr/dot_general | solution.py:45
  175.6 0.1 constant_dynamic-slice_fusion.2
  175.7 19.5 %fusion.39 = f32[64,1024]{1,0:T(8,128)S(1)} fusion(f32[1024]{0:T(1024)S(1)} %bitcast.24, f32[4096]{0:T(1024)S(1)} %bitcast.22, f32[1024]{0:T(1024)S(1)} %bitcast.23, f32[4096]{0:T(1024)S(1)} %bitcast.21, f32[64,32768]{1,0:T(8,128)} %get-tuple-element.190, s32[]{:T(128)S(6)} %select_n.14, f32[64,1024]{1,0:T(8,128)S(1)} %get-tuple-element.179, ...), kind=kOutput, calls=%fused_computation.15.clone.1 | convolution fusion | flops 3250716672 | bytes 1613829 | tf_op jit(solution)/shard_map/while/body/eval_jaxpr/dot_general | solution.py:45
  195.3 0.1 constant_dynamic-slice_fusion.2
  195.4 19.5 %fusion.39 = f32[64,1024]{1,0:T(8,128)S(1)} fusion(f32[1024]{0:T(1024)S(1)} %bitcast.24, f32[4096]{0:T(1024)S(1)} %bitcast.22, f32[1024]{0:T(1024)S(1)} %bitcast.23, f32[4096]{0:T(1024)S(1)} %bitcast.21, f32[64,32768]{1,0:T(8,128)} %get-tuple-element.190, s32[]{:T(128)S(6)} %select_n.14, f32[64,1024]{1,0:T(8,128)S(1)} %get-tuple-element.179, ...), kind=kOutput, calls=%fused_computation.15.clone.1 | convolution fusion | flops 3250716672 | bytes 1613829 | tf_op jit(solution)/shard_map/while/body/eval_jaxpr/dot_general | solution.py:45
  214.9 0.1 constant_dynamic-slice_fusion.2
  215.0 19.5 %fusion.39 = f32[64,1024]{1,0:T(8,128)S(1)} fusion(f32[1024]{0:T(1024)S(1)} %bitcast.24, f32[4096]{0:T(1024)S(1)} %bitcast.22, f32[1024]{0:T(1024)S(1)} %bitcast.23, f32[4096]{0:T(1024)S(1)} %bitcast.21, f32[64,32768]{1,0:T(8,128)} %get-tuple-element.190, s32[]{:T(128)S(6)} %select_n.14, f32[64,1024]{1,0:T(8,128)S(1)} %get-tuple-element.179, ...), kind=kOutput, calls=%fused_computation.15.clone.1 | convolution fusion | flops 3250716672 | bytes 1613829 | tf_op jit(solution)/shard_map/while/body/eval_jaxpr/dot_general | solution.py:45
  234.6 0.1 constant_dynamic-slice_fusion.2
  234.7 19.5 %fusion.39 = f32[64,1024]{1,0:T(8,128)S(1)} fusion(f32[1024]{0:T(1024)S(1)} %bitcast.24, f32[4096]{0:T(1024)S(1)} %bitcast.22, f32[1024]{0:T(1024)S(1)} %bitcast.23, f32[4096]{0:T(1024)S(1)} %bitcast.21, f32[64,32768]{1,0:T(8,128)} %get-tuple-element.190, s32[]{:T(128)S(6)} %select_n.14, f32[64,1024]{1,0:T(8,128)S(1)} %get-tuple-element.179, ...), kind=kOutput, calls=%fused_computation.15.clone.1 | convolution fusion | flops 3250716672 | bytes 1613829 | tf_op jit(solution)/shard_map/while/body/eval_jaxpr/dot_general | solution.py:45
  254.2 0.1 constant_dynamic-slice_fusion.2
  254.3 19.5 %fusion.39 = f32[64,1024]{1,0:T(8,128)S(1)} fusion(f32[1024]{0:T(1024)S(1)} %bitcast.24, f32[4096]{0:T(1024)S(1)} %bitcast.22, f32[1024]{0:T(1024)S(1)} %bitcast.23, f32[4096]{0:T(1024)S(1)} %bitcast.21, f32[64,32768]{1,0:T(8,128)} %get-tuple-element.190, s32[]{:T(128)S(6)} %select_n.14, f32[64,1024]{1,0:T(8,128)S(1)} %get-tuple-element.179, ...), kind=kOutput, calls=%fused_computation.15.clone.1 | convolution fusion | flops 3250716672 | bytes 1613829 | tf_op jit(solution)/shard_map/while/body/eval_jaxpr/dot_general | solution.py:45
  274.0 0.1 reshape.52
  274.2 0.8 copy.16
  275.0 0.0 all-gather.9.cloned.1.call-start
  275.1 48.3 %all-gather.7.cloned.1.call-done = f32[32,16,1024]{2,0,1:T(8,128)} async-done(((f32[32,2,1024]{2,0,1:T(8,128)}), f32[32,16,1024]{2,0,1:T(8,128)}) %all-gather.7.cloned.1.call-update) | async-done | bytes 2097168 | tf_op jit(solution)/shard_map/all_gather | solution.py:51
  323.4 3.9 fusion.23
  327.3 1.1 convolution_bitcast_fusion
  328.4 719.7 %all-gather.9.cloned.1.call-done = f32[8192,32]{1,0:T(8,128)} async-done(((f32[32,32]{1,0:T(8,128)}), f32[8192,32]{1,0:T(8,128)}) %all-gather.9.cloned.1.call-update) | async-done | bytes 1048592 | tf_op jit(solution)/shard_map/all_gather | solution.py:55
  1048.1 3.1 reduce_sum.9
  (19 shorter events, 0.2 us)
Async XLA Ops:
  7.2 316.2 %copy-start = (f32[16,16]{1,0:T(8,128)S(1)}, f32[16,16]{1,0:T(8,128)}, u32[]{:S(2)}) copy-start(f32[16,16]{1,0:T(8,128)} %param.9) | copy-start | bytes 3076
  7.2 109.5 %all-gather.5.cloned.1.call-start = ((), (), s32[]{:S(2)}) async-start(), calls=%async_computation | async-start | bytes 8650752 | tf_op jit(solution)/shard_map/all_gather | solution.py:35
  10.1 313.3 %all-gather.7.cloned.1.call-start = ((), (), s32[]{:S(2)}) async-start(), calls=%async_computation.1 | async-start | bytes 2359296 | tf_op jit(solution)/shard_map/all_gather | solution.py:51
  275.0 773.1 %all-gather.9.cloned.1.call-start = ((), (), s32[]{:S(2)}) async-start(), calls=%async_computation.2 | async-start | bytes 4210688 | tf_op jit(solution)/shard_map/all_gather | solution.py:55
  327.3 724.0 %copy-start.1 = (f32[32,2,1024]{2,1,0:T(2,128)}, f32[32,2,1024]{2,1,0:T(2,128)S(1)}, u32[]{:S(2)}) copy-start(f32[32,2,1024]{2,1,0:T(2,128)S(1)} %fusion.23) | copy-start | bytes 786436
Sparse Core Ops, SparseCore 0:
  11.4 105.2 all-gather.4
  275.1 48.2 all-gather.6
  328.5 719.5 all-gather.8
